TPU v7x, 128 devices: a whole 4x4x4 slice. The times are simulated.
128 devices in a mesh: region: 32 (over x, z, core), basis: 4 (over y).
Axes of the slice: x: 4, y: 4, z: 4, core: 2. Of those that a mesh axis runs over, the one named last changes fastest.
Arguments:
- observations: bfloat16 [1048576, 128], P(('region', 'basis')), may hold values from -3 to 4
- basis_values: bfloat16 [1048576, 1024], P(('region', 'basis')), as said below
- mixing: bfloat16 [1024, 1024], P('basis'), may hold values from -0.1875 to 0.1875
- pattern: int32 [8, 8], replicated, may hold values 0 or 1
- decays: float32 [32, 1024], P('region', 'basis'), may hold values from 0 to 1
- loadings: float32 [1024], P('basis'), may hold values from 0.3 to 3
Outputs:
- obs_grad: bfloat16 [1048576, 128], P(('region', 'basis'))
- attenuation_slope: float32 [32, 1024], P('region', 'basis')
Inputs may be any that keep to these rules, and one draw needn't show every extreme that they name: `basis_values`: every entry lies within 3.5 / 32768 ** 0.5 of zero.
All inputs are finite; a program needn't handle non-finite values.
Results may differ from a plain program's by a relative error of at most 0.015.
Values may be sent and summed in bfloat16 or wider, within the bound.
No kernel may reach another device: no remote copies, remote signals or barrier semaphores. Data moves between devices by JAX's collectives and lax.ppermute only.
A program may use at most 128 MiB of HBM per device.

v0:
```python
import jax
import jax.numpy as jnp
from jax import lax
from jax.sharding import PartitionSpec as P

BLOCK = 128


def entering(value, axis, join, neutral, backward):
    count, mine = (lax.axis_size(axis), lax.axis_index(axis))
    pieces = jax.tree.map(lambda part: lax.all_gather(part, axis), value)
    if backward:
        pieces = jax.tree.map(lambda part: part[::-1], pieces)
        mine = count - 1 - mine
    subtotal = jax.tree.map(
        lambda part, zero: jnp.full_like(part, 0) + jnp.asarray(zero, part.dtype), value, neutral
    )

    def turn(position, subtotal):
        longer = join(subtotal, jax.tree.map(lambda part: part[position], pieces))
        return jax.tree.map(lambda new, old: jnp.where(position < mine, new, old), longer, subtotal)

    return lax.fori_loop(0, count - 1, turn, subtotal)


def contract_rows(first_operand, second_operand):
    return lax.dot_general(
        first_operand, second_operand, (((0,), (0,)), ((), ())), preferred_element_type=jnp.float32
    )


def block_rows(mixing, pattern, owner):
    row_count = mixing.shape[0]
    width = mixing.shape[1]
    row_ids = owner * row_count + jnp.arange(row_count)
    column_index = jnp.arange(width)
    labels = jnp.arange(pattern.shape[0])
    row_hot = ((row_ids // BLOCK)[:, None] == labels[None, :]).astype(jnp.float32)
    column_hot = ((column_index // BLOCK)[:, None] == labels[None, :]).astype(jnp.float32)
    expanded = jnp.dot(jnp.dot(row_hot, pattern.astype(jnp.float32)), column_hot.T)
    identity = (row_ids[:, None] == column_index[None, :]).astype(jnp.float32)
    return (identity + mixing.astype(jnp.float32) * expanded).astype(jnp.bfloat16)


def combine(earlier, later):
    return (earlier[0] * later[0], later[0][:, None] * earlier[1] + later[1])


def shards(observations, basis_values, mixing, pattern, decays, loadings):
    owner = lax.axis_index("basis")
    share = mixing.shape[0]
    characteristics = observations.shape[1]
    mixer_rows = block_rows(mixing, pattern, owner)
    rates = decays[0]
    zero_share = jnp.zeros((share, characteristics), jnp.float32)
    identity_pair = (jnp.ones((share,), jnp.float32), zero_share)

    def predict_piece(piece):
        return jnp.dot(basis_values, piece, preferred_element_type=jnp.float32)

    summary = lax.psum_scatter(
        contract_rows(basis_values, observations), "basis", scatter_dimension=0, tiled=True
    )
    mixed_terms = jnp.dot(
        mixer_rows,
        lax.all_gather(summary.astype(jnp.bfloat16), "basis", axis=0, tiled=True),
        preferred_element_type=jnp.float32,
    )
    _, previous = entering((rates, mixed_terms), "region", combine, identity_pair, False)
    states = rates[:, None] * previous + mixed_terms
    loaded_values = (loadings[:, None] * states).astype(jnp.bfloat16)
    fitted = predict_piece(lax.all_gather(loaded_values, "basis", axis=0, tiled=True))
    residual = (fitted - observations.astype(jnp.float32)).astype(jnp.bfloat16)
    pulled = loadings[:, None] * lax.psum_scatter(
        contract_rows(basis_values, residual).astype(jnp.bfloat16),
        "basis",
        scatter_dimension=0,
        tiled=True,
    ).astype(jnp.float32)
    _, carried = entering((rates, rates[:, None] * pulled), "region", combine, identity_pair, True)
    adjoints = pulled + carried
    attenuation_slope = (jnp.sum(adjoints * previous, axis=1) / characteristics)[None, :]
    adjoint_b = adjoints.astype(jnp.bfloat16)
    back_owned = lax.psum_scatter(
        contract_rows(mixer_rows, adjoint_b), "basis", scatter_dimension=0, tiled=True
    ).astype(jnp.bfloat16)
    spread = predict_piece(lax.all_gather(back_owned, "basis", axis=0, tiled=True))
    obs_grad = (spread - residual.astype(jnp.float32)).astype(jnp.bfloat16)
    return (obs_grad, attenuation_slope)


def solution(mesh):
    in_specs = (
        P(("region", "basis"), None),
        P(("region", "basis"), None),
        P("basis", None),
        P(),
        P("region", "basis"),
        P("basis"),
    )
    out_specs = (P(("region", "basis"), None), P("region", "basis"))
    return jax.shard_map(shards, mesh=mesh, in_specs=in_specs, out_specs=out_specs, check_vma=False)
```

profile of v0, /device:TPU:0, one launch (start us, length us, event | category | flops | bytes accessed | tf_op | source)
XLA Modules:
  0.0 337.9 jit_solution(7736925620875022976)
XLA Ops:
  7.2 11.7 %fusion.25 = f32[1024,128]{1,0:T(8,128)} fusion(bf16[8192,1024]{1,0:T(8,128)(2,1)} %param.11, bf16[8192,128]{1,0:T(8,128)(2,1)} %param.10), kind=kOutput, calls=%fused_computation.46 | convolution fusion | flops 2147483648 | bytes 19398656 | tf_op jit(solution)/shard_map/dot_general | solution.py:27
  19.0 1.7 fusion.7
  20.7 22.3 %reduce-scatter.4.cloned.1.call-done = f32[256,128]{1,0:T(8,128)} async-done(((f32[1024,128]{1,0:T(8,128)}), f32[256,128]{1,0:T(8,128)}) %reduce-scatter.4.cloned.1.call-update) | async-done | bytes 131088 | tf_op jit(solution)/shard_map/reduce_scatter | solution.py:61
  43.9 12.2 %all_gather.26 = bf16[1024,128]{1,0:T(8,128)(2,1)S(1)} all-gather(bf16[256,128]{1,0:T(8,128)(2,1)S(1)} %convert_element_type.51), channel_id=1, replica_groups=mesh['region'=32,'basis'=4] {'basis'}, dimensions={0}, use_global_device_ids=true | all-gather | bytes 327680 | tf_op jit(solution)/shard_map/all_gather | solution.py:66
  57.2 2.9 copy.11
  60.1 24.3 %all-gather.2 = f32[32,1,256]{2,1,0:T(1,128)S(1)} all-gather(f32[1,1,256]{2,1,0:T(1,128)S(1)} %bitcast.56), channel_id=1, replica_groups=mesh['region'=32,'basis'=4] {'region'}, dimensions={0}, use_global_device_ids=true | all-gather | bytes 33792 | tf_op jit(solution)/shard_map/all_gather | solution.py:11
  84.4 19.0 %all-gather.6.cloned.1.call-done = f32[8192,128]{1,0:T(8,128)} async-done(((f32[256,128]{1,0:T(8,128)}), f32[8192,128]{1,0:T(8,128)}) %all-gather.6.cloned.1.call-update) | async-done | bytes 4194320 | tf_op jit(solution)/shard_map/all_gather | solution.py:11
  103.4 33.2 %while.28 = (s32[]{:T(128)}, f32[256,128]{1,0:T(8,128)S(1)}, s32[]{:T(128)}, f32[32,256]{1,0:T(8,128)S(1)}, f32[32,256,128]{2,1,0:T(8,128)}, /*index=5*/s32[]{:T(128)}, s32[]{:T(128)}) while((s32[]{:T(128)}, f32[256,128]{1,0:T(8,128)S(1)}, s32[]{:T(128)}, f32[32,256]{1,0:T(8,128)S(1)}, f32[32,256,128]{2,1,0:T(8,128)}, ...), condition=%wide.region_2.3_spmd.clone, body=%wide.region_1.2_spmd.clone.sunk | while | flops 131076 | bytes 396393 | solution.py:23
  104.4 1.0 fusion.40
  105.5 1.0 fusion.40
  106.6 1.0 fusion.40
  107.7 1.0 fusion.40
  108.7 1.0 fusion.40
  109.8 1.0 fusion.40
  110.9 1.0 fusion.40
  111.9 1.0 fusion.40
  113.0 1.0 fusion.40
  114.1 1.0 fusion.40
  115.2 1.0 fusion.40
  116.2 1.0 fusion.40
  117.3 1.0 fusion.40
  118.4 1.0 fusion.40
  119.4 1.0 fusion.40
  120.5 1.0 fusion.40
  121.6 1.0 fusion.40
  122.7 1.0 fusion.40
  123.7 1.0 fusion.40
  124.8 1.0 fusion.40
  125.9 1.0 fusion.40
  126.9 1.0 fusion.40
  128.0 1.0 fusion.40
  129.1 1.0 fusion.40
  130.2 1.0 fusion.40
  134.4 1.0 fusion.40
  136.7 12.8 %all_gather.29 = bf16[1024,128]{1,0:T(8,128)(2,1)S(1)} all-gather(bf16[256,128]{1,0:T(8,128)(2,1)S(1)} %multiply_convert_fusion), channel_id=1, replica_groups=mesh['region'=32,'basis'=4] {'basis'}, dimensions={0}, use_global_device_ids=true | all-gather | bytes 327680 | tf_op jit(solution)/shard_map/all_gather | solution.py:72
  149.5 12.0 %fusion.5 = bf16[8192,128]{0,1:T(8,128)(2,1)S(1)} fusion(bf16[1024,128]{1,0:T(8,128)(2,1)S(1)} %all_gather.29, bf16[8192,1024]{1,0:T(8,128)(2,1)} %param.11, bf16[8192,128]{0,1:T(8,128)(2,1)} %copy.11), kind=kOutput, calls=%fused_computation.11 | convolution fusion | flops 2150629376 | bytes 21233664 | tf_op jit(solution)/shard_map/dot_general | solution.py:59
  161.5 10.8 %fusion.8 = bf16[1024,128]{1,0:T(8,128)(2,1)} fusion(bf16[8192,128]{0,1:T(8,128)(2,1)S(1)} %fusion.5, bf16[8192,1024]{1,0:T(8,128)(2,1)} %param.11), kind=kOutput, calls=%fused_computation.16 | convolution fusion | flops 2147614720 | bytes 19136512 | tf_op jit(solution)/shard_map/dot_general | solution.py:27
  172.4 19.7 %reduce-scatter.6.cloned.1.call-done = bf16[256,128]{1,0:T(8,128)(2,1)} async-done(((bf16[1024,128]{1,0:T(8,128)(2,1)}), bf16[256,128]{1,0:T(8,128)(2,1)}) %reduce-scatter.6.cloned.1.call-update) | async-done | bytes 65552 | tf_op jit(solution)/shard_map/reduce_scatter | solution.py:74
  192.1 1.6 fusion.13
  193.9 47.3 %all-gather.8.cloned.1.call-done = f32[8192,128]{1,0:T(8,128)} async-done(((f32[256,128]{1,0:T(8,128)}), f32[8192,128]{1,0:T(8,128)}) %all-gather.8.cloned.1.call-update) | async-done | bytes 4194320 | tf_op jit(solution)/shard_map/all_gather | solution.py:11
  241.2 4.6 %rev.7 = f32[32,256,128]{2,1,0:T(8,128)} reverse(f32[32,256,128]{2,1,0:T(8,128)} %bitcast.51), dimensions={0} | reverse | bytes 8388608 | tf_op jit(solution)/shard_map/rev | solution.py:13
  245.9 33.2 %while.29 = (s32[]{:T(128)}, f32[256,128]{1,0:T(8,128)S(1)}, s32[]{:T(128)}, f32[32,256]{1,0:T(8,128)S(1)}, f32[32,256,128]{2,1,0:T(8,128)}, /*index=5*/s32[]{:T(128)}, s32[]{:T(128)}) while((s32[]{:T(128)}, f32[256,128]{1,0:T(8,128)S(1)}, s32[]{:T(128)}, f32[32,256]{1,0:T(8,128)S(1)}, f32[32,256,128]{2,1,0:T(8,128)}, ...), condition=%wide.region_5.6_spmd.clone, body=%wide.region_4.5_spmd.clone.sunk | while | flops 131076 | bytes 396393 | solution.py:23
  260.9 1.0 fusion.41
  279.1 1.2 fusion.15
  281.0 20.1 %reduce-scatter.8.cloned.1.call-done = f32[256,128]{1,0:T(8,128)} async-done(((f32[1024,128]{1,0:T(8,128)}), f32[256,128]{1,0:T(8,128)}) %reduce-scatter.8.cloned.1.call-update) | async-done | bytes 131088 | tf_op jit(solution)/shard_map/reduce_scatter | solution.py:84
  302.1 12.5 %all_gather.32 = bf16[1024,128]{1,0:T(8,128)(2,1)S(1)} all-gather(bf16[256,128]{1,0:T(8,128)(2,1)S(1)} %convert_element_type.59), channel_id=1, replica_groups=mesh['region'=32,'basis'=4] {'basis'}, dimensions={0}, use_global_device_ids=true | all-gather | bytes 327680 | tf_op jit(solution)/shard_map/all_gather | solution.py:87
  314.5 12.8 %fusion.4 = bf16[8192,128]{0,1:T(8,128)(2,1)} fusion(bf16[1024,128]{1,0:T(8,128)(2,1)S(1)} %all_gather.32, bf16[8192,1024]{1,0:T(8,128)(2,1)} %param.11, bf16[8192,128]{0,1:T(8,128)(2,1)S(1)} %fusion.5), kind=kOutput, calls=%fused_computation.10 | convolution fusion | flops 2150629376 | bytes 21233664 | tf_op jit(solution)/shard_map/dot_general | solution.py:59
  327.3 4.1 %copy.13 = bf16[8192,128]{1,0:T(8,128)(2,1)} copy(bf16[8192,128]{0,1:T(8,128)(2,1)} %fusion.4) | data formatting | bytes 4194304
  (131 shorter events, 40.6 us)
Async XLA Ops:
  7.2 11.8 %copy-start.5 = (s32[8,8]{1,0:T(8,128)S(1)}, s32[8,8]{1,0:T(8,128)}, u32[]{:S(2)}) copy-start(s32[8,8]{1,0:T(8,128)} %param.13) | copy-start | bytes 772
  7.2 35.8 %reduce-scatter.4.cloned.1.call-start = ((), (), s32[]{:S(2)}) async-start(), calls=%async_computation.3 | async-start | bytes 655360 | tf_op jit(solution)/shard_map/reduce_scatter | solution.py:61
  18.9 38.3 %copy-start = (bf16[8192,128]{1,0:T(8,128)(2,1)S(1)}, bf16[8192,128]{1,0:T(8,128)(2,1)}, u32[]{:S(2)}) copy-start(bf16[8192,128]{1,0:T(8,128)(2,1)} %param.10) | copy-start | bytes 6291460
  18.9 41.2 %copy-start.4 = (f32[1,256]{1,0:T(1,128)S(1)}, f32[1,256]{1,0:T(1,128)}, u32[]{:S(2)}) copy-start(f32[1,256]{1,0:T(1,128)} %param.14) | copy-start | bytes 3076
  18.9 84.4 %all-gather.6.cloned.1.call-start = ((), (), s32[]{:S(2)}) async-start(), calls=%async_computation.6 | async-start | bytes 4325376 | tf_op jit(solution)/shard_map/all_gather | solution.py:11
  20.7 115.9 %copy-start.3 = (f32[256]{0:T(256)S(1)}, f32[256]{0:T(256)}, u32[]{:S(2)}) copy-start(f32[256]{0:T(256)} %param.15) | copy-start | bytes 3076
  57.1 79.5 %copy-start.1 = (f32[256,128]{1,0:T(8,128)S(1)}, f32[256,128]{1,0:T(8,128)}, u32[]{:S(2)}) copy-start(f32[256,128]{1,0:T(8,128)} %fusion.26) | copy-start | bytes 393220
  57.1 135.1 %reduce-scatter.6.cloned.1.call-start = ((), (), s32[]{:S(2)}) async-start(), calls=%async_computation.4 | async-start | bytes 327680 | tf_op jit(solution)/shard_map/reduce_scatter | solution.py:74
  172.4 68.8 %all-gather.8.cloned.1.call-start = ((), (), s32[]{:S(2)}) async-start(), calls=%async_computation.7 | async-start | bytes 4325376 | tf_op jit(solution)/shard_map/all_gather | solution.py:11
  193.8 107.4 %reduce-scatter.8.cloned.1.call-start = ((), (), s32[]{:S(2)}) async-start(), calls=%async_computation.5 | async-start | bytes 655360 | tf_op jit(solution)/shard_map/reduce_scatter | solution.py:84
  241.2 37.8 %copy-start.2 = (bf16[256,128]{1,0:T(8,128)(2,1)S(1)}, bf16[256,128]{1,0:T(8,128)(2,1)}, u32[]{:S(2)}) copy-start(bf16[256,128]{1,0:T(8,128)(2,1)} %reduce-scatter.6.cloned.1.call-done) | copy-start | bytes 196612
Sparse Core Ops, SparseCore 0:
  19.0 23.8 reduce-scatter.3
  57.2 46.1 all-gather.5
  172.5 19.6 reduce-scatter.5
  195.1 46.0 all-gather.7
  280.4 20.7 reduce-scatter.7
where the time goes:
time: 339 us; the launch traced here: 338 us
  waiting for transfers between devices  128 us (38%)
  other arithmetic  68.1 us (20%)
  blocking collectives  61.8 us (18%)
  matrix products  51.1 us (15%)
  between operations  13.9 us (4%)
  local copies, waits for them, and re-layouts  12.3 us (4%)
    all_gather x2, waiting for transfers between devices, entering(): pieces = jax.tree.map(lambda part: lax.all_gather(part, axis), value)  66.3 us
    select_n x62, other arithmetic, turn(): jnp.where(position < mine, new, old)  63.8 us
    dot_general x2, matrix products, predict_piece(): return jnp.dot(basis_values, piece, preferred_element_type=jnp.float32)  24.8 us
    all_gather x1, blocking collectives, entering(): pieces = jax.tree.map(lambda part: lax.all_gather(part, axis), value)  24.3 us
    dot_general x3, matrix products, contract_rows(): lax.dot_general(first_operand, second_operand, (((0,), (0,)), ((), ())),...  23.7 us
    reduce_scatter x1, waiting for transfers between devices, shards(): lax.psum_scatter(contract_rows(basis_values, observations), 'basis', scat...  22.3 us
    reduce_scatter x1, waiting for transfers between devices, shards(): lax.psum_scatter(contract_rows(mixer_rows, adjoint_b), 'basis', scatter_d...  20.1 us
    reduce_scatter x1, waiting for transfers between devices, shards(): lax.psum_scatter(contract_rows(basis_values, residual).astype(jnp.bfloat1...  19.7 us
  transfers between devices with their start and end apart: 5, of which 5 were waited for; matrix products, arithmetic and copies ran while one was open for 2% of the time, Pallas kernels for 0%

commit v1 on v0

--- a/solution.py
+++ b/solution.py
@@ -63,7 +63,12 @@
     )
     mixed_terms = jnp.dot(
         mixer_rows,
-        lax.all_gather(summary.astype(jnp.bfloat16), "basis", axis=0, tiled=True),
+        jnp.concatenate(
+            lax.all_to_all(
+                jnp.stack([summary.astype(jnp.bfloat16)] * lax.axis_size("basis")), "basis", 0, 0
+            ),
+            axis=0,
+        ),
         preferred_element_type=jnp.float32,
     )
     _, previous = entering((rates, mixed_terms), "region", combine, identity_pair, False)

time: 339 us -> 338 us (level)
  blocking collectives: 61.8 us -> 49.6 us
  waiting for transfers between devices: 128 us -> 135 us
  starting transfers between devices: 0.21 us -> 3.61 us
    all_gather x1 -> x0, blocking collectives: 12.2 us -> none  [shards(): lax.all_gather(summary.astype(jnp.bfloat16), 'basis', axis=0, tiled=True)]
    all_to_all x0 -> x1, waiting for transfers between devices: none -> 5.02 us  [shards(): lax.all_to_all(jnp.stack([summary.astype(jnp.bfloat16)] * lax.axis_size('...]
    all_to_all x0 -> x1, starting transfers between devices: none -> 3.41 us  [shards(): lax.all_to_all(jnp.stack([summary.astype(jnp.bfloat16)] * lax.axis_size('...]
  transfers between devices with their start and end apart: 5 -> 6, of which waited for: 5 -> 6; matrix products, arithmetic and copies ran while one was open for 2% -> 2% of each run, Pallas kernels for 0% -> 0%
where the time goes in v1:
time: 338 us; the launch traced here: 336 us
  waiting for transfers between devices  135 us (40%)
  other arithmetic  68.1 us (20%)
  matrix products  51 us (15%)
  blocking collectives  49.6 us (15%)
  between operations  13.9 us (4%)
  local copies, waits for them, and re-layouts  13 us (4%)
  starting transfers between devices  3.61 us (1%)
    all_gather x2, waiting for transfers between devices, entering(): pieces = jax.tree.map(lambda part: lax.all_gather(part, axis), value)  66 us
    select_n x62, other arithmetic, turn(): jnp.where(position < mine, new, old)  63.8 us
    dot_general x2, matrix products, predict_piece(): return jnp.dot(basis_values, piece, preferred_element_type=jnp.float32)  24.8 us
    all_gather x1, blocking collectives, entering(): pieces = jax.tree.map(lambda part: lax.all_gather(part, axis), value)  24.3 us
    reduce_scatter x1, waiting for transfers between devices, shards(): lax.psum_scatter(contract_rows(basis_values, observations), 'basis', scat...  24 us
    dot_general x3, matrix products, contract_rows(): lax.dot_general(first_operand, second_operand, (((0,), (0,)), ((), ())),...  23.7 us
    reduce_scatter x1, waiting for transfers between devices, shards(): lax.psum_scatter(contract_rows(mixer_rows, adjoint_b), 'basis', scatter_d...  20.1 us
    reduce_scatter x1, waiting for transfers between devices, shards(): lax.psum_scatter(contract_rows(basis_values, residual).astype(jnp.bfloat1...  19.7 us
  transfers between devices with their start and end apart: 6, of which 6 were waited for; matrix products, arithmetic and copies ran while one was open for 2% of the time, Pallas kernels for 0%

profile of v1, /device:TPU:0, one launch (start us, length us, event | category | flops | bytes accessed | tf_op | source)
XLA Modules:
  0.0 336.2 jit_solution(9158178683526068367)
XLA Ops:
  7.2 11.7 %fusion.25 = f32[1024,128]{1,0:T(8,128)} fusion(bf16[8192,1024]{1,0:T(8,128)(2,1)} %param.11, bf16[8192,128]{1,0:T(8,128)(2,1)} %param.10), kind=kOutput, calls=%fused_computation.46 | convolution fusion | flops 2147483648 | bytes 19398656 | tf_op jit(solution)/shard_map/dot_general | solution.py:27
  19.0 24.0 %reduce-scatter.4.cloned.1.call-done = f32[256,128]{1,0:T(8,128)} async-done(((f32[1024,128]{1,0:T(8,128)}), f32[256,128]{1,0:T(8,128)}) %reduce-scatter.4.cloned.1.call-update) | async-done | bytes 131088 | tf_op jit(solution)/shard_map/reduce_scatter | solution.py:61
  44.6 3.4 %all-to-all-start = ((bf16[4,256,128]{2,1,0:T(8,128)(2,1)}), bf16[4,256,128]{2,1,0:T(8,128)(2,1)S(1)}, u32[]{:S(2)}, u32[]{:S(2)}) async-start(bf16[4,256,128]{2,1,0:T(8,128)(2,1)} %stack.2), calls=%async_computation.1 | async-start | bytes 524288 | tf_op jit(solution)/shard_map/all_to_all | solution.py:67
  48.1 1.5 fusion.7
  49.7 5.0 %all-to-all-done = bf16[4,256,128]{2,1,0:T(8,128)(2,1)S(1)} async-done(((bf16[4,256,128]{2,1,0:T(8,128)(2,1)}), bf16[4,256,128]{2,1,0:T(8,128)(2,1)S(1)}, u32[]{:S(2)}, u32[]{:S(2)}) %all-to-all-start) | async-done | bytes 262176 | tf_op jit(solution)/shard_map/all_to_all | solution.py:67
  55.7 2.9 copy.11
  58.6 24.3 %all-gather.2 = f32[32,1,256]{2,1,0:T(1,128)S(1)} all-gather(f32[1,1,256]{2,1,0:T(1,128)S(1)} %bitcast.58), channel_id=1, replica_groups=mesh['region'=32,'basis'=4] {'region'}, dimensions={0}, use_global_device_ids=true | all-gather | bytes 33792 | tf_op jit(solution)/shard_map/all_gather | solution.py:11
  82.9 18.7 %all-gather.6.cloned.1.call-done = f32[8192,128]{1,0:T(8,128)} async-done(((f32[256,128]{1,0:T(8,128)}), f32[8192,128]{1,0:T(8,128)}) %all-gather.6.cloned.1.call-update) | async-done | bytes 4194320 | tf_op jit(solution)/shard_map/all_gather | solution.py:11
  101.6 33.2 %while.28 = (s32[]{:T(128)}, f32[256,128]{1,0:T(8,128)S(1)}, s32[]{:T(128)}, f32[32,256]{1,0:T(8,128)S(1)}, f32[32,256,128]{2,1,0:T(8,128)}, /*index=5*/s32[]{:T(128)}, s32[]{:T(128)}) while((s32[]{:T(128)}, f32[256,128]{1,0:T(8,128)S(1)}, s32[]{:T(128)}, f32[32,256]{1,0:T(8,128)S(1)}, f32[32,256,128]{2,1,0:T(8,128)}, ...), condition=%wide.region_2.3_spmd.clone, body=%wide.region_1.2_spmd.clone.sunk | while | flops 131076 | bytes 396393 | solution.py:23
  102.7 1.0 fusion.40
  103.8 1.0 fusion.40
  104.8 1.0 fusion.40
  105.9 1.0 fusion.40
  107.0 1.0 fusion.40
  108.1 1.0 fusion.40
  109.1 1.0 fusion.40
  110.2 1.0 fusion.40
  111.3 1.0 fusion.40
  112.3 1.0 fusion.40
  113.4 1.0 fusion.40
  114.5 1.0 fusion.40
  115.6 1.0 fusion.40
  116.6 1.0 fusion.40
  117.7 1.0 fusion.40
  118.8 1.0 fusion.40
  119.8 1.0 fusion.40
  120.9 1.0 fusion.40
  122.0 1.0 fusion.40
  123.1 1.0 fusion.40
  124.1 1.0 fusion.40
  125.2 1.0 fusion.40
  126.3 1.0 fusion.40
  127.3 1.0 fusion.40
  135.0 12.8 %all_gather.25 = bf16[1024,128]{1,0:T(8,128)(2,1)S(1)} all-gather(bf16[256,128]{1,0:T(8,128)(2,1)S(1)} %multiply_convert_fusion), channel_id=1, replica_groups=mesh['region'=32,'basis'=4] {'basis'}, dimensions={0}, use_global_device_ids=true | all-gather | bytes 327680 | tf_op jit(solution)/shard_map/all_gather | solution.py:77
  147.7 12.0 %fusion.5 = bf16[8192,128]{0,1:T(8,128)(2,1)S(1)} fusion(bf16[1024,128]{1,0:T(8,128)(2,1)S(1)} %all_gather.25, bf16[8192,1024]{1,0:T(8,128)(2,1)} %param.11, bf16[8192,128]{0,1:T(8,128)(2,1)} %copy.11), kind=kOutput, calls=%fused_computation.11 | convolution fusion | flops 2150629376 | bytes 21233664 | tf_op jit(solution)/shard_map/dot_general | solution.py:59
  159.8 10.8 %fusion.8 = bf16[1024,128]{1,0:T(8,128)(2,1)} fusion(bf16[8192,128]{0,1:T(8,128)(2,1)S(1)} %fusion.5, bf16[8192,1024]{1,0:T(8,128)(2,1)} %param.11), kind=kOutput, calls=%fused_computation.16 | convolution fusion | flops 2147614720 | bytes 19136512 | tf_op jit(solution)/shard_map/dot_general | solution.py:27
  170.7 19.7 %reduce-scatter.6.cloned.1.call-done = bf16[256,128]{1,0:T(8,128)(2,1)} async-done(((bf16[1024,128]{1,0:T(8,128)(2,1)}), bf16[256,128]{1,0:T(8,128)(2,1)}) %reduce-scatter.6.cloned.1.call-update) | async-done | bytes 65552 | tf_op jit(solution)/shard_map/reduce_scatter | solution.py:79
  190.4 1.6 fusion.13
  192.2 47.3 %all-gather.8.cloned.1.call-done = f32[8192,128]{1,0:T(8,128)} async-done(((f32[256,128]{1,0:T(8,128)}), f32[8192,128]{1,0:T(8,128)}) %all-gather.8.cloned.1.call-update) | async-done | bytes 4194320 | tf_op jit(solution)/shard_map/all_gather | solution.py:11
  239.5 4.6 %rev.7 = f32[32,256,128]{2,1,0:T(8,128)} reverse(f32[32,256,128]{2,1,0:T(8,128)} %bitcast.52), dimensions={0} | reverse | bytes 8388608 | tf_op jit(solution)/shard_map/rev | solution.py:13
  244.1 33.2 %while.29 = (s32[]{:T(128)}, f32[256,128]{1,0:T(8,128)S(1)}, s32[]{:T(128)}, f32[32,256]{1,0:T(8,128)S(1)}, f32[32,256,128]{2,1,0:T(8,128)}, /*index=5*/s32[]{:T(128)}, s32[]{:T(128)}) while((s32[]{:T(128)}, f32[256,128]{1,0:T(8,128)S(1)}, s32[]{:T(128)}, f32[32,256]{1,0:T(8,128)S(1)}, f32[32,256,128]{2,1,0:T(8,128)}, ...), condition=%wide.region_5.6_spmd.clone, body=%wide.region_4.5_spmd.clone.sunk | while | flops 131076 | bytes 396393 | solution.py:23
  250.5 1.0 fusion.41
  270.9 1.0 fusion.41
  277.3 1.2 fusion.15
  279.3 20.1 %reduce-scatter.8.cloned.1.call-done = f32[256,128]{1,0:T(8,128)} async-done(((f32[1024,128]{1,0:T(8,128)}), f32[256,128]{1,0:T(8,128)}) %reduce-scatter.8.cloned.1.call-update) | async-done | bytes 131088 | tf_op jit(solution)/shard_map/reduce_scatter | solution.py:89
  300.3 12.5 %all_gather.28 = bf16[1024,128]{1,0:T(8,128)(2,1)S(1)} all-gather(bf16[256,128]{1,0:T(8,128)(2,1)S(1)} %convert_element_type.59), channel_id=1, replica_groups=mesh['region'=32,'basis'=4] {'basis'}, dimensions={0}, use_global_device_ids=true | all-gather | bytes 327680 | tf_op jit(solution)/shard_map/all_gather | solution.py:92
  312.8 12.8 %fusion.4 = bf16[8192,128]{0,1:T(8,128)(2,1)} fusion(bf16[1024,128]{1,0:T(8,128)(2,1)S(1)} %all_gather.28, bf16[8192,1024]{1,0:T(8,128)(2,1)} %param.11, bf16[8192,128]{0,1:T(8,128)(2,1)S(1)} %fusion.5), kind=kOutput, calls=%fused_computation.10 | convolution fusion | flops 2150629376 | bytes 21233664 | tf_op jit(solution)/shard_map/dot_general | solution.py:59
  325.6 4.1 %copy.13 = bf16[8192,128]{1,0:T(8,128)(2,1)} copy(bf16[8192,128]{0,1:T(8,128)(2,1)} %fusion.4) | data formatting | bytes 4194304
  (133 shorter events, 42.4 us)
Async XLA Ops:
  7.2 40.9 %copy-start.5 = (s32[8,8]{1,0:T(8,128)S(1)}, s32[8,8]{1,0:T(8,128)}, u32[]{:S(2)}) copy-start(s32[8,8]{1,0:T(8,128)} %param.13) | copy-start | bytes 772
  7.2 35.8 %reduce-scatter.4.cloned.1.call-start = ((), (), s32[]{:S(2)}) async-start(), calls=%async_computation.4 | async-start | bytes 655360 | tf_op jit(solution)/shard_map/reduce_scatter | solution.py:61
  18.9 36.8 %copy-start = (bf16[8192,128]{1,0:T(8,128)(2,1)S(1)}, bf16[8192,128]{1,0:T(8,128)(2,1)}, u32[]{:S(2)}) copy-start(bf16[8192,128]{1,0:T(8,128)(2,1)} %param.10) | copy-start | bytes 6291460
  18.9 39.7 %copy-start.4 = (f32[1,256]{1,0:T(1,128)S(1)}, f32[1,256]{1,0:T(1,128)}, u32[]{:S(2)}) copy-start(f32[1,256]{1,0:T(1,128)} %param.14) | copy-start | bytes 3076
  44.6 10.1 %all-to-all-start = ((bf16[4,256,128]{2,1,0:T(8,128)(2,1)}), bf16[4,256,128]{2,1,0:T(8,128)(2,1)S(1)}, u32[]{:S(2)}, u32[]{:S(2)}) async-start(bf16[4,256,128]{2,1,0:T(8,128)(2,1)} %stack.2), calls=%async_computation.1 | async-start | bytes 524288 | tf_op jit(solution)/shard_map/all_to_all | solution.py:67
  48.0 53.6 %all-gather.6.cloned.1.call-start = ((), (), s32[]{:S(2)}) async-start(), calls=%async_computation.7 | async-start | bytes 4325376 | tf_op jit(solution)/shard_map/all_gather | solution.py:11
  48.1 86.7 %copy-start.3 = (f32[256]{0:T(256)S(1)}, f32[256]{0:T(256)}, u32[]{:S(2)}) copy-start(f32[256]{0:T(256)} %param.15) | copy-start | bytes 3076
  55.6 79.2 %copy-start.1 = (f32[256,128]{1,0:T(8,128)S(1)}, f32[256,128]{1,0:T(8,128)}, u32[]{:S(2)}) copy-start(f32[256,128]{1,0:T(8,128)} %fusion.26) | copy-start | bytes 393220
  55.6 134.8 %reduce-scatter.6.cloned.1.call-start = ((), (), s32[]{:S(2)}) async-start(), calls=%async_computation.5 | async-start | bytes 327680 | tf_op jit(solution)/shard_map/reduce_scatter | solution.py:79
  170.6 68.8 %all-gather.8.cloned.1.call-start = ((), (), s32[]{:S(2)}) async-start(), calls=%async_computation.8 | async-start | bytes 4325376 | tf_op jit(solution)/shard_map/all_gather | solution.py:11
  192.1 107.4 %reduce-scatter.8.cloned.1.call-start = ((), (), s32[]{:S(2)}) async-start(), calls=%async_computation.6 | async-start | bytes 655360 | tf_op jit(solution)/shard_map/reduce_scatter | solution.py:89
  239.5 37.9 %copy-start.2 = (bf16[256,128]{1,0:T(8,128)(2,1)S(1)}, bf16[256,128]{1,0:T(8,128)(2,1)}, u32[]{:S(2)}) copy-start(bf16[256,128]{1,0:T(8,128)(2,1)} %reduce-scatter.6.cloned.1.call-done) | copy-start | bytes 196612
Sparse Core Ops, SparseCore 0:
  19.0 23.8 reduce-scatter.3
  55.8 45.8 all-gather.5
  170.7 19.6 reduce-scatter.5
  193.3 46.0 all-gather.7
  278.7 20.7 reduce-scatter.7
